TPU v7x, 512 devices: a whole 4x8x8 slice. The times are simulated.
512 devices in a mesh: elem: 32 (over y_lo, z), orb: 16 (over x, y_hi, core).
Axes of the slice: x: 4, y: 8 (y_hi: 2, y_lo: 4; y = y_hi * 4 + y_lo), z: 8, core: 2. Of those that a mesh axis runs over, the one named last changes fastest.
Arguments:
- orbitals: bfloat16 [24576, 4096], P('elem', 'orb')
- hamiltonian: bfloat16 [384, 7, 64, 64], P('elem'), may hold values from -0.25 to 0.25
- neighbours: int32 [384, 7], P('elem'), may hold values from 0 to 383, as said below
Outputs:
- updated: bfloat16 [24576, 4096], P('elem', 'orb')
Inputs may be any that keep to these rules, and one draw needn't show every extreme that they name: Elements form tiles of 12 consecutive indices, each tile a periodic 3 x 4 plane of elements in some order, tiles stacked periodically. An element's row lists itself, its two neighbours along each in-plane direction, then the element at the same place in the previous tile and in the next tile.
All inputs are finite; a program needn't handle non-finite values.
Results may differ from a plain program's by a relative error of at most 0.0062.
Values may be sent and summed in bfloat16 or wider, within the bound.
A program may use at most 64 MiB of HBM per device.

v0:
```python
import jax
import jax.numpy as jnp
from jax import lax
from jax.sharding import PartitionSpec as P


def extended_2(value, sides, width):
    for axis, dim in sides:
        peers, length = (lax.axis_size(axis), value.shape[dim])
        up = [(i, (i + 1) % peers) for i in range(peers)]
        down = [(j, i) for i, j in up]
        last = lax.slice_in_dim(value, length - width, length, axis=dim)
        initial = lax.slice_in_dim(value, 0, width, axis=dim)
        before = lax.ppermute(last, axis, up)
        after = lax.ppermute(initial, axis, down)
        value = jnp.concatenate([before, value, after], axis=dim)
    return value


def neighbour_product(hamiltonian, local_index, field):
    rows, width = field.shape
    elements = hamiltonian.shape[0]
    block_size = hamiltonian.shape[2]
    extended = extended_2(field, (("elem", 0),), rows)
    blocks = extended.reshape(3 * elements, block_size, width)
    picked = blocks[local_index]
    result = jnp.einsum("enab,enbc->eac", hamiltonian, picked, preferred_element_type=jnp.float32)
    return result.reshape(rows, width)


def local(orbitals, hamiltonian, neighbours):
    elements = hamiltonian.shape[0]
    tiles = lax.axis_size("elem")
    my_tile = lax.axis_index("elem")
    other_tile = neighbours // elements
    relative = (other_tile - my_tile + tiles) % tiles
    slot = jnp.where(relative == 0, 1, jnp.where(relative == 1, 2, 0)).astype(jnp.int32)
    local_index = slot * elements + neighbours % elements
    start_field = orbitals.astype(jnp.float32)
    first = neighbour_product(hamiltonian, local_index, orbitals)
    first_half = first.astype(jnp.bfloat16)
    second = 2.0 * neighbour_product(hamiltonian, local_index, first_half) - start_field
    second_half = second.astype(jnp.bfloat16)
    third = 2.0 * neighbour_product(hamiltonian, local_index, second_half) - first
    filtered = third.astype(jnp.bfloat16)
    rows_total = filtered.shape[0] * tiles
    columns = filtered.shape[1]
    groups = lax.axis_size("orb")
    my_group = lax.axis_index("orb")
    orbital_count = columns * groups
    panel = lax.all_gather(filtered, "orb", axis=1, tiled=True)
    partial_gram = lax.dot_general(
        panel, filtered, (((0,), (0,)), ((), ())), preferred_element_type=jnp.float32
    )
    gram_part = lax.psum_scatter(partial_gram, "elem", scatter_dimension=0, tiled=True)
    share = gram_part.shape[0]
    row_global = my_tile * share + lax.broadcasted_iota(jnp.int32, gram_part.shape, 0)
    col_global = my_group * columns + lax.broadcasted_iota(jnp.int32, gram_part.shape, 1)
    own_diagonal = jnp.sum(jnp.where(row_global == col_global, gram_part, 0.0))
    total = lax.psum(own_diagonal, ("elem", "orb"))
    level = total / (orbital_count * rows_total)
    scaled_part = (gram_part / (level * rows_total)).astype(jnp.bfloat16)
    scaled = lax.all_gather(scaled_part, "elem", axis=0, tiled=True)
    mixed = jnp.dot(panel, scaled, preferred_element_type=jnp.float32)
    result = (1.5 * filtered.astype(jnp.float32) - 0.5 * mixed) / jnp.sqrt(level)
    return result.astype(jnp.bfloat16)


def solution(mesh):
    return jax.shard_map(
        local,
        mesh=mesh,
        in_specs=(P("elem", "orb"), P("elem", None, None, None), P("elem", None)),
        out_specs=P("elem", "orb"),
        check_vma=False,
    )
```

profile of v0, /device:TPU:2, one launch (start us, length us, event | category | flops | bytes accessed | tf_op | source)
XLA Modules:
  0.0 612.7 jit_solution(15075717939295863914)
XLA Ops:
  6.5 4.4 collective-permute-start
  10.9 11.6 %collective-permute-start.1 = (bf16[768,256]{1,0:T(8,128)(2,1)}, bf16[768,256]{1,0:T(8,128)(2,1)S(1)}, u32[]{:S(2)}, u32[]{:S(2)}) collective-permute-start(bf16[768,256]{1,0:T(8,128)(2,1)} %param.3), channel_id=1, source_target_pairs={{16,0},{32,16},{48,32},{64,48},{80,64},{96,80},{112,96},{128,112},... | collective-permute-start | bytes 1179656 | tf_op jit(solution)/shard_map/ppermute | solution.py:15
  22.6 0.7 compare_select_fusion
  23.3 0.1 copy.5
  23.4 0.1 reshape.24
  23.5 6.5 %collective-permute-done = bf16[768,256]{1,0:T(8,128)(2,1)S(1)} collective-permute-done((bf16[768,256]{1,0:T(8,128)(2,1)}, bf16[768,256]{1,0:T(8,128)(2,1)S(1)}, u32[]{:S(2)}, u32[]{:S(2)}) %collective-permute-start) | collective-permute-done | bytes 393248 | tf_op jit(solution)/shard_map/ppermute | solution.py:14
  30.0 1.3 collective-permute-done.1
  31.3 1.1 pad_maximum_fusion
  32.3 2.4 gather_fusion
  34.8 2.4 fusion.13
  37.2 1.9 collective-permute-start.2
  39.1 8.2 %collective-permute-start.3 = (bf16[768,256]{1,0:T(8,128)(2,1)S(1)}, bf16[768,256]{1,0:T(8,128)(2,1)S(1)}, u32[]{:S(2)}, u32[]{:S(2)}) collective-permute-start(bf16[768,256]{1,0:T(8,128)(2,1)S(1)} %bitcast.52), channel_id=1, source_target_pairs={{16,0},{32,16},{48,32},{64,48},{80,64},{96,80},{112,96},{128,112},... | collective-permute-start | bytes 1179656 | tf_op jit(solution)/shard_map/ppermute | solution.py:15
  47.3 6.3 %collective-permute-done.2 = bf16[768,256]{1,0:T(8,128)(2,1)S(1)} collective-permute-done((bf16[768,256]{1,0:T(8,128)(2,1)S(1)}, bf16[768,256]{1,0:T(8,128)(2,1)S(1)}, u32[]{:S(2)}, u32[]{:S(2)}) %collective-permute-start.2) | collective-permute-done | bytes 393248 | tf_op jit(solution)/shard_map/ppermute | solution.py:14
  53.6 1.2 collective-permute-done.3
  54.8 0.1 pad_maximum_fusion.1
  54.9 2.4 gather_fusion.1
  57.3 2.4 fusion.2
  59.8 0.1 fusion.7
  59.9 1.9 collective-permute-start.4
  61.8 8.3 %collective-permute-start.5 = (bf16[768,256]{1,0:T(8,128)(2,1)S(1)}, bf16[768,256]{1,0:T(8,128)(2,1)S(1)}, u32[]{:S(2)}, u32[]{:S(2)}) collective-permute-start(bf16[768,256]{1,0:T(8,128)(2,1)S(1)} %fusion.7), channel_id=1, source_target_pairs={{16,0},{32,16},{48,32},{64,48},{80,64},{96,80},{112,96},{128,112},... | collective-permute-start | bytes 1179656 | tf_op jit(solution)/shard_map/ppermute | solution.py:15
  70.1 5.5 collective-permute-done.4
  75.6 1.2 collective-permute-done.5
  76.8 2.4 gather_fusion.2
  79.3 3.1 fusion.4
  82.5 91.5 %all-gather.3.cloned.1.call-done = bf16[768,4096]{1,0:T(8,128)(2,1)} async-done(((bf16[768,256]{1,0:T(8,128)(2,1)}), bf16[768,4096]{1,0:T(8,128)(2,1)}) %all-gather.3.cloned.1.call-update) | async-done | bytes 6291472 | tf_op jit(solution)/shard_map/all_gather | solution.py:51
  174.0 6.7 %fusion.14 = f32[4096,256]{1,0:T(8,128)} fusion(bf16[768,4096]{1,0:T(8,128)(2,1)} %all-gather.3.cloned.1.call-done, bf16[768,256]{1,0:T(8,128)(2,1)} %bitcast.55), kind=kOutput, calls=%fused_computation.37 | convolution fusion | flops 1610612736 | bytes 10878976 | tf_op jit(solution)/shard_map/dot_general | solution.py:52
  180.8 172.7 %reduce-scatter.2.cloned.1.call-done = f32[128,256]{1,0:T(8,128)} async-done(((f32[4096,256]{1,0:T(8,128)}), f32[128,256]{1,0:T(8,128)}) %reduce-scatter.2.cloned.1.call-update) | async-done | bytes 131088 | tf_op jit(solution)/shard_map/reduce_scatter | solution.py:55
  353.5 1.6 select_reduce_fusion
  355.1 93.4 %psum.7 = f32[]{:T(128)} all-reduce(f32[]{:T(128)} %select_reduce_fusion), channel_id=1, replica_groups=mesh['elem'=32,'orb'=16] {'elem','orb'}, use_global_device_ids=true, to_apply=%region_2.3 | all-reduce | flops 1 | bytes 8 | tf_op jit(solution)/shard_map/psum | solution.py:60
  449.1 1.5 divide_convert_fusion
  451.2 149.0 %all-gather.5.cloned.1.call-done = bf16[4096,256]{1,0:T(8,128)(2,1)} async-done(((bf16[128,256]{1,0:T(8,128)(2,1)}), bf16[4096,256]{1,0:T(8,128)(2,1)}) %all-gather.5.cloned.1.call-update) | async-done | bytes 2097168 | tf_op jit(solution)/shard_map/all_gather | solution.py:63
  600.3 6.0 fusion.6
  (16 shorter events, 0.2 us)
Async XLA Ops:
  6.5 28.2 %copy-start = (bf16[12,7,64,64]{3,2,1,0:T(8,128)(2,1)S(1)}, bf16[12,7,64,64]{3,2,1,0:T(8,128)(2,1)}, u32[]{:S(2)}) copy-start(bf16[12,7,64,64]{3,2,1,0:T(8,128)(2,1)} %param.4) | copy-start | bytes 2064388
  6.5 167.4 %all-gather.3.cloned.1.call-start = ((), (), s32[]{:S(2)}) async-start(), calls=%async_computation.1 | async-start | bytes 6684672 | tf_op jit(solution)/shard_map/all_gather | solution.py:51
  6.5 23.4 %collective-permute-start = (bf16[768,256]{1,0:T(8,128)(2,1)}, bf16[768,256]{1,0:T(8,128)(2,1)S(1)}, u32[]{:S(2)}, u32[]{:S(2)}) collective-permute-start(bf16[768,256]{1,0:T(8,128)(2,1)} %param.3), channel_id=1, source_target_pairs={{0,16},{16,32},{32,48},{48,64},{64,80},{80,96},{96,112},{112,128},... | collective-permute-start | bytes 1179656 | tf_op jit(solution)/shard_map/ppermute | solution.py:14
  10.9 20.3 %collective-permute-start.1 = (bf16[768,256]{1,0:T(8,128)(2,1)}, bf16[768,256]{1,0:T(8,128)(2,1)S(1)}, u32[]{:S(2)}, u32[]{:S(2)}) collective-permute-start(bf16[768,256]{1,0:T(8,128)(2,1)} %param.3), channel_id=1, source_target_pairs={{16,0},{32,16},{48,32},{64,48},{80,64},{96,80},{112,96},{128,112},... | collective-permute-start | bytes 1179656 | tf_op jit(solution)/shard_map/ppermute | solution.py:15
  37.2 16.4 %collective-permute-start.2 = (bf16[768,256]{1,0:T(8,128)(2,1)S(1)}, bf16[768,256]{1,0:T(8,128)(2,1)S(1)}, u32[]{:S(2)}, u32[]{:S(2)}) collective-permute-start(bf16[768,256]{1,0:T(8,128)(2,1)S(1)} %bitcast.51), channel_id=1, source_target_pairs={{0,16},{16,32},{32,48},{48,64},{64,80},{80,96},{96,112},{112,128},... | collective-permute-start | bytes 1179656 | tf_op jit(solution)/shard_map/ppermute | solution.py:14
  39.1 15.7 %collective-permute-start.3 = (bf16[768,256]{1,0:T(8,128)(2,1)S(1)}, bf16[768,256]{1,0:T(8,128)(2,1)S(1)}, u32[]{:S(2)}, u32[]{:S(2)}) collective-permute-start(bf16[768,256]{1,0:T(8,128)(2,1)S(1)} %bitcast.52), channel_id=1, source_target_pairs={{16,0},{32,16},{48,32},{64,48},{80,64},{96,80},{112,96},{128,112},... | collective-permute-start | bytes 1179656 | tf_op jit(solution)/shard_map/ppermute | solution.py:15
  57.3 2.4 copy-start.1
  59.9 15.7 %collective-permute-start.4 = (bf16[768,256]{1,0:T(8,128)(2,1)S(1)}, bf16[768,256]{1,0:T(8,128)(2,1)S(1)}, u32[]{:S(2)}, u32[]{:S(2)}) collective-permute-start(bf16[768,256]{1,0:T(8,128)(2,1)S(1)} %fusion.7), channel_id=1, source_target_pairs={{0,16},{16,32},{32,48},{48,64},{64,80},{80,96},{96,112},{112,128},... | collective-permute-start | bytes 1179656 | tf_op jit(solution)/shard_map/ppermute | solution.py:14
  61.8 14.9 %collective-permute-start.5 = (bf16[768,256]{1,0:T(8,128)(2,1)S(1)}, bf16[768,256]{1,0:T(8,128)(2,1)S(1)}, u32[]{:S(2)}, u32[]{:S(2)}) collective-permute-start(bf16[768,256]{1,0:T(8,128)(2,1)S(1)} %fusion.7), channel_id=1, source_target_pairs={{16,0},{32,16},{48,32},{64,48},{80,64},{96,80},{112,96},{128,112},... | collective-permute-start | bytes 1179656 | tf_op jit(solution)/shard_map/ppermute | solution.py:15
  82.4 271.1 %reduce-scatter.2.cloned.1.call-start = ((), (), s32[]{:S(2)}) async-start(), calls=%async_computation.2 | async-start | bytes 4325376 | tf_op jit(solution)/shard_map/reduce_scatter | solution.py:55
  180.7 419.6 %copy-start.2 = (bf16[12,256,64]{1,2,0:T(8,128)(2,1)S(1)}, bf16[12,256,64]{1,2,0:T(8,128)(2,1)}, u32[]{:S(2)}) copy-start(bf16[12,256,64]{1,2,0:T(8,128)(2,1)} %fusion.4) | copy-start | bytes 1179652
  180.7 419.6 %all-gather.5.cloned.1.call-start = ((), (), s32[]{:S(2)}) async-start(), calls=%async_computation.3 | async-start | bytes 2162688 | tf_op jit(solution)/shard_map/all_gather | solution.py:63
Sparse Core Ops, SparseCore 0:
  82.5 91.4 all-gather.2
  180.8 172.6 reduce-scatter.1
  450.7 149.4 all-gather.4
where the time goes:
time: 613 us
  waiting for transfers between devices  435 us (71%)
  blocking collectives  93.4 us (15%)
  starting transfers between devices  36.4 us (6%)
  matrix products  20.6 us (3%)
  between operations  14.4 us (2%)
  local copies, waits for them, and re-layouts  7.51 us (1%)
    reduce_scatter x1, waiting for transfers between devices, local(): lax.psum_scatter(partial_gram, 'elem', scatter_dimension=0, tiled=True)  173 us
    all_gather x1, waiting for transfers between devices, local(): scaled = lax.all_gather(scaled_part, 'elem', axis=0, tiled=True)  149 us
    psum x1, blocking collectives, local(): total = lax.psum(own_diagonal, ('elem', 'orb'))  93.4 us
    all_gather x1, waiting for transfers between devices, local(): panel = lax.all_gather(filtered, 'orb', axis=1, tiled=True)  91.5 us
    ppermute x3, starting transfers between devices, extended_2(): after = lax.ppermute(initial, axis, down)  28.1 us
    ppermute x3, waiting for transfers between devices, extended_2(): before = lax.ppermute(last, axis, up)  18.2 us
  transfers between devices with their start and end apart: 9, of which 9 were waited for; matrix products, arithmetic and copies ran while one was open for 0% of the time, Pallas kernels for 0%

commit v1 on v0

--- a/solution.py
+++ b/solution.py
@@ -2,6 +2,7 @@
 import jax.numpy as jnp
 from jax import lax
 from jax.sharding import PartitionSpec as P
+from jax.lax import all_to_all, psum
 
 
 def extended_2(value, sides, width):
@@ -48,7 +49,15 @@
     groups = lax.axis_size("orb")
     my_group = lax.axis_index("orb")
     orbital_count = columns * groups
-    panel = lax.all_gather(filtered, "orb", axis=1, tiled=True)
+    panel = jnp.concatenate(
+        all_to_all(
+            jnp.stack([filtered] * psum(1, axis_name="orb")),
+            axis_name="orb",
+            split_axis=0,
+            concat_axis=0,
+        ),
+        axis=1,
+    )
     partial_gram = lax.dot_general(
         panel, filtered, (((0,), (0,)), ((), ())), preferred_element_type=jnp.float32
     )

time: 613 us -> 663 us (1.082)
  blocking collectives: 93.4 us -> 236 us
  waiting for transfers between devices: 435 us -> 341 us
    all_to_all x0 -> x1, blocking collectives: none -> 144 us  [local(): all_to_all(jnp.stack([filtered] * psum(1, axis_name='orb')), axis_name='o...]
    all_gather x1 -> x0, waiting for transfers between devices: 91.5 us -> none  [local(): panel = lax.all_gather(filtered, 'orb', axis=1, tiled=True)]
  transfers between devices with their start and end apart: 9 -> 8, of which waited for: 9 -> 8; matrix products, arithmetic and copies ran while one was open for 0% -> 0% of each run, Pallas kernels for 0% -> 0%
where the time goes in v1:
time: 663 us; the launch traced here: 662 us
  waiting for transfers between devices  341 us (51%)
  blocking collectives  236 us (36%)
  starting transfers between devices  36.4 us (5%)
  matrix products  17.1 us (3%)
  between operations  14.9 us (2%)
  local copies, waits for them, and re-layouts  10.9 us (2%)
    reduce_scatter x1, waiting for transfers between devices, local(): lax.psum_scatter(partial_gram, 'elem', scatter_dimension=0, tiled=True)  170 us
    all_gather x1, waiting for transfers between devices, local(): scaled = lax.all_gather(scaled_part, 'elem', axis=0, tiled=True)  150 us
    all_to_all x1, blocking collectives, local(): all_to_all(jnp.stack([filtered] * psum(1, axis_name='orb')), axis_name='o...  144 us
    psum x1, blocking collectives, local(): total = lax.psum(own_diagonal, ('elem', 'orb'))  92.2 us
    ppermute x3, starting transfers between devices, extended_2(): after = lax.ppermute(initial, axis, down)  28.1 us
    ppermute x3, waiting for transfers between devices, extended_2(): before = lax.ppermute(last, axis, up)  18.2 us
  transfers between devices with their start and end apart: 8, of which 8 were waited for; matrix products, arithmetic and copies ran while one was open for 0% of the time, Pallas kernels for 0%

profile of v1, /device:TPU:2, one launch (start us, length us, event | category | flops | bytes accessed | tf_op | source)
XLA Modules:
  0.0 662.0 jit_solution(8316823797213717524)
XLA Ops:
  6.5 4.4 collective-permute-start
  10.9 11.6 %collective-permute-start.1 = (bf16[768,256]{1,0:T(8,128)(2,1)}, bf16[768,256]{1,0:T(8,128)(2,1)S(1)}, u32[]{:S(2)}, u32[]{:S(2)}) collective-permute-start(bf16[768,256]{1,0:T(8,128)(2,1)} %param.3), channel_id=1, source_target_pairs={{16,0},{32,16},{48,32},{64,48},{80,64},{96,80},{112,96},{128,112},... | collective-permute-start | bytes 1179656 | tf_op jit(solution)/shard_map/ppermute | solution.py:16
  22.6 0.7 compare_select_fusion
  23.3 0.1 copy.5
  23.5 6.5 collective-permute-done
  30.0 1.3 collective-permute-done.1
  31.3 1.1 pad_maximum_fusion
  32.3 2.4 gather_fusion
  34.8 2.4 fusion.13
  37.2 1.9 collective-permute-start.2
  39.1 8.2 %collective-permute-start.3 = (bf16[768,256]{1,0:T(8,128)(2,1)S(1)}, bf16[768,256]{1,0:T(8,128)(2,1)S(1)}, u32[]{:S(2)}, u32[]{:S(2)}) collective-permute-start(bf16[768,256]{1,0:T(8,128)(2,1)S(1)} %bitcast.60), channel_id=1, source_target_pairs={{16,0},{32,16},{48,32},{64,48},{80,64},{96,80},{112,96},{128,112},... | collective-permute-start | bytes 1179656 | tf_op jit(solution)/shard_map/ppermute | solution.py:16
  47.3 6.3 collective-permute-done.2
  53.6 1.2 collective-permute-done.3
  54.9 2.4 gather_fusion.1
  57.3 2.4 fusion.2
  59.9 1.9 collective-permute-start.4
  61.8 8.3 %collective-permute-start.5 = (bf16[768,256]{1,0:T(8,128)(2,1)S(1)}, bf16[768,256]{1,0:T(8,128)(2,1)S(1)}, u32[]{:S(2)}, u32[]{:S(2)}) collective-permute-start(bf16[768,256]{1,0:T(8,128)(2,1)S(1)} %fusion.7), channel_id=1, source_target_pairs={{16,0},{32,16},{48,32},{64,48},{80,64},{96,80},{112,96},{128,112},... | collective-permute-start | bytes 1179656 | tf_op jit(solution)/shard_map/ppermute | solution.py:16
  70.1 5.5 collective-permute-done.4
  75.6 1.2 collective-permute-done.5
  76.8 2.4 gather_fusion.2
  79.2 2.4 fusion.4
  81.6 0.2 copy.6
  81.8 0.6 stack.2
  82.4 143.9 %all_to_all.5 = bf16[16,768,256]{1,2,0:T(8,128)(2,1)S(1)} all-to-all(bf16[16,768,256]{1,2,0:T(8,128)(2,1)S(1)} %stack.2), channel_id=1, replica_groups=mesh['elem'=32,'orb'=16] {'orb'}, dimensions={0} | all-to-all | bytes 12582912 | tf_op jit(solution)/shard_map/all_to_all | solution.py:53
  226.3 2.7 copy-done.1
  229.0 3.9 fusion.14
  233.0 169.6 %reduce-scatter.2.cloned.1.call-done = f32[128,256]{1,0:T(8,128)} async-done(((f32[4096,256]{1,0:T(8,128)}), f32[128,256]{1,0:T(8,128)}) %reduce-scatter.2.cloned.1.call-update) | async-done | bytes 131088 | tf_op jit(solution)/shard_map/reduce_scatter | solution.py:64
  402.5 1.6 select_reduce_fusion
  404.2 92.2 %psum.7 = f32[]{:T(128)} all-reduce(f32[]{:T(128)} %select_reduce_fusion), channel_id=1, replica_groups=mesh['elem'=32,'orb'=16] {'elem','orb'}, use_global_device_ids=true, to_apply=%region_2.3 | all-reduce | flops 1 | bytes 8 | tf_op jit(solution)/shard_map/psum | solution.py:69
  497.1 1.6 divide_convert_fusion
  499.3 149.8 %all-gather.2.cloned.1.call-done = bf16[4096,256]{1,0:T(8,128)(2,1)} async-done(((bf16[128,256]{1,0:T(8,128)(2,1)}), bf16[4096,256]{1,0:T(8,128)(2,1)}) %all-gather.2.cloned.1.call-update) | async-done | bytes 2097168 | tf_op jit(solution)/shard_map/all_gather | solution.py:72
  649.1 6.0 fusion.6
  (16 shorter events, 0.4 us)
Async XLA Ops:
  6.5 28.2 %copy-start = (bf16[12,7,64,64]{3,2,1,0:T(8,128)(2,1)S(1)}, bf16[12,7,64,64]{3,2,1,0:T(8,128)(2,1)}, u32[]{:S(2)}) copy-start(bf16[12,7,64,64]{3,2,1,0:T(8,128)(2,1)} %param.4) | copy-start | bytes 2064388
  6.5 396.0 %reduce-scatter.2.cloned.1.call-start = ((), (), s32[]{:S(2)}) async-start(), calls=%async_computation.2 | async-start | bytes 4325376 | tf_op jit(solution)/shard_map/reduce_scatter | solution.py:64
  6.5 23.4 %collective-permute-start = (bf16[768,256]{1,0:T(8,128)(2,1)}, bf16[768,256]{1,0:T(8,128)(2,1)S(1)}, u32[]{:S(2)}, u32[]{:S(2)}) collective-permute-start(bf16[768,256]{1,0:T(8,128)(2,1)} %param.3), channel_id=1, source_target_pairs={{0,16},{16,32},{32,48},{48,64},{64,80},{80,96},{96,112},{112,128},... | collective-permute-start | bytes 1179656 | tf_op jit(solution)/shard_map/ppermute | solution.py:15
  10.9 20.3 %collective-permute-start.1 = (bf16[768,256]{1,0:T(8,128)(2,1)}, bf16[768,256]{1,0:T(8,128)(2,1)S(1)}, u32[]{:S(2)}, u32[]{:S(2)}) collective-permute-start(bf16[768,256]{1,0:T(8,128)(2,1)} %param.3), channel_id=1, source_target_pairs={{16,0},{32,16},{48,32},{64,48},{80,64},{96,80},{112,96},{128,112},... | collective-permute-start | bytes 1179656 | tf_op jit(solution)/shard_map/ppermute | solution.py:16
  37.2 16.4 %collective-permute-start.2 = (bf16[768,256]{1,0:T(8,128)(2,1)S(1)}, bf16[768,256]{1,0:T(8,128)(2,1)S(1)}, u32[]{:S(2)}, u32[]{:S(2)}) collective-permute-start(bf16[768,256]{1,0:T(8,128)(2,1)S(1)} %bitcast.59), channel_id=1, source_target_pairs={{0,16},{16,32},{32,48},{48,64},{64,80},{80,96},{96,112},{112,128},... | collective-permute-start | bytes 1179656 | tf_op jit(solution)/shard_map/ppermute | solution.py:15
  39.1 15.7 %collective-permute-start.3 = (bf16[768,256]{1,0:T(8,128)(2,1)S(1)}, bf16[768,256]{1,0:T(8,128)(2,1)S(1)}, u32[]{:S(2)}, u32[]{:S(2)}) collective-permute-start(bf16[768,256]{1,0:T(8,128)(2,1)S(1)} %bitcast.60), channel_id=1, source_target_pairs={{16,0},{32,16},{48,32},{64,48},{80,64},{96,80},{112,96},{128,112},... | collective-permute-start | bytes 1179656 | tf_op jit(solution)/shard_map/ppermute | solution.py:16
  57.3 2.4 copy-start.2
  59.9 15.7 %collective-permute-start.4 = (bf16[768,256]{1,0:T(8,128)(2,1)S(1)}, bf16[768,256]{1,0:T(8,128)(2,1)S(1)}, u32[]{:S(2)}, u32[]{:S(2)}) collective-permute-start(bf16[768,256]{1,0:T(8,128)(2,1)S(1)} %fusion.7), channel_id=1, source_target_pairs={{0,16},{16,32},{32,48},{48,64},{64,80},{80,96},{96,112},{112,128},... | collective-permute-start | bytes 1179656 | tf_op jit(solution)/shard_map/ppermute | solution.py:15
  61.8 14.9 %collective-permute-start.5 = (bf16[768,256]{1,0:T(8,128)(2,1)S(1)}, bf16[768,256]{1,0:T(8,128)(2,1)S(1)}, u32[]{:S(2)}, u32[]{:S(2)}) collective-permute-start(bf16[768,256]{1,0:T(8,128)(2,1)S(1)} %fusion.7), channel_id=1, source_target_pairs={{16,0},{32,16},{48,32},{64,48},{80,64},{96,80},{112,96},{128,112},... | collective-permute-start | bytes 1179656 | tf_op jit(solution)/shard_map/ppermute | solution.py:16
  226.3 2.7 copy-start.1
  232.9 416.3 %all-gather.2.cloned.1.call-start = ((), (), s32[]{:S(2)}) async-start(), calls=%async_computation.3 | async-start | bytes 2162688 | tf_op jit(solution)/shard_map/all_gather | solution.py:72
Sparse Core Ops, SparseCore 0:
  233.0 169.4 reduce-scatter.1
  498.8 150.3 all-gather.1
